TPU v7x, 32 devices: a whole 2x2x4 slice. The times are simulated.
32 devices in a mesh: seq: 4 (over z), head: 8 (over y, x, core).
Axes of the slice: x: 2, y: 2, z: 4, core: 2. Of those that a mesh axis runs over, the one named last changes fastest.
Arguments:
- query: float32 [3072, 1024], P('seq', 'head'), may hold values from -6 to 6
- key_in: float32 [3072, 1024], P('seq', 'head'), may hold values from -6 to 6
- value: float32 [3072, 1024], P('seq', 'head'), may hold values from -6 to 6
- out_grad: float32 [3072, 1024], P('seq', 'head'), may hold values from -6 to 6
- head_scale: float32 [8], P('head'), may hold values from 0.5 to 2
- norm_gain: float32 [1024], P('head'), may hold values from 0.5 to 1.5
- group_counts: int32 [4], replicated, may hold values from 1 to 6, 12 in all
Outputs:
- normed: float32 [3072, 1024], P('seq', 'head')
- grad_query: float32 [3072, 1024], P('seq', 'head')
- grad_key: float32 [3072, 1024], P('seq', 'head')
- grad_value: float32 [3072, 1024], P('seq', 'head')
Inputs may be any that keep to these rules, and one draw needn't show every extreme that they name: The live rows of shard i are its first 128 * group_counts[i] rows; the counts sum to 3 * 4 and the largest is exactly 6.
All inputs are finite; a program needn't handle non-finite values.
Results may differ from a plain program's by a relative error of at most 0.0001.
Values sent between devices are 32-bit elements; how exact they have to be, the bound alone decides.
A program may use at most 64 MiB of HBM per device.

v0:
```python
import jax
import jax.numpy as jnp
from jax import lax
from jax.sharding import PartitionSpec as P

GROUP = 128


def plain_product(left, right):
    return jnp.dot(left, right, precision=lax.Precision.HIGHEST, preferred_element_type=jnp.float32)


def leading_product(left, right):
    return lax.dot_general(
        left,
        right,
        (((0,), (0,)), ((), ())),
        precision=lax.Precision.HIGHEST,
        preferred_element_type=jnp.float32,
    )


def on_device(query, key_in, value, out_grad, head_scale, norm_gain, group_counts):
    capacity, features_dev = query.shape
    shard_pos = lax.axis_index("seq")
    block_live = group_counts[shard_pos]
    live_rows = (jnp.arange(capacity) < block_live * GROUP)[:, None]
    q_rows = jnp.where(live_rows, query, 0.0)
    k_rows = jnp.where(live_rows, key_in, 0.0)
    v_rows = jnp.where(live_rows, value, 0.0)
    causal = jnp.tril(jnp.ones((GROUP, GROUP), dtype=bool))
    block_total = capacity // GROUP
    zero_state = jnp.zeros((features_dev, features_dev), jnp.float32)

    def forward_step(block_idx, state_pack):
        running, outputs, saved_states, saved_scores = state_pack
        row_start = block_idx * GROUP
        q_block = lax.dynamic_slice_in_dim(q_rows, row_start, GROUP, 0)
        k_block = lax.dynamic_slice_in_dim(k_rows, row_start, GROUP, 0)
        v_block = lax.dynamic_slice_in_dim(v_rows, row_start, GROUP, 0)
        scores = jnp.where(causal, plain_product(q_block, k_block.T), 0.0)
        local_part = plain_product(q_block, running) + plain_product(scores, v_block)
        outputs = lax.dynamic_update_slice_in_dim(outputs, local_part, row_start, 0)
        saved_states = lax.dynamic_update_index_in_dim(saved_states, running, block_idx, 0)
        saved_scores = lax.dynamic_update_index_in_dim(saved_scores, scores, block_idx, 0)
        running = running + leading_product(k_block, v_block)
        return (running, outputs, saved_states, saved_scores)

    forward_init = (
        zero_state,
        jnp.zeros((capacity, features_dev), jnp.float32),
        jnp.zeros((block_total, features_dev, features_dev), jnp.float32),
        jnp.zeros((block_total, GROUP, GROUP), jnp.float32),
    )
    shard_state, local_out, saved_states, saved_scores = lax.fori_loop(
        0, block_live, forward_step, forward_init
    )
    piece_rows = lax.all_gather(shard_state[None], "seq", axis=0, tiled=True)
    picked = (jnp.arange(piece_rows.shape[0]) < shard_pos)[:, None, None]
    state_in = jnp.sum(jnp.where(picked, piece_rows, 0.0), axis=0)
    attended = local_out + plain_product(q_rows, state_in)
    scaled = attended * head_scale[0]
    features = features_dev * lax.axis_size("head")
    squares, cross_terms = lax.psum(
        (jnp.sum(scaled * scaled, axis=1), jnp.sum(norm_gain[None, :] * out_grad * scaled, axis=1)),
        "head",
    )
    inverse = lax.rsqrt(squares / features + 1e-05)[:, None]
    normed = scaled * inverse * norm_gain[None, :]
    grad_scaled = (
        inverse * norm_gain[None, :] * out_grad
        - scaled * inverse * inverse * inverse * cross_terms[:, None] / features
    )
    grad_out = grad_scaled * head_scale[0]

    def backward_step(step_idx, state_pack):
        running, grad_q, grad_k, grad_v = state_pack
        block_idx = block_live - 1 - step_idx
        row_start = block_idx * GROUP
        q_block = lax.dynamic_slice_in_dim(q_rows, row_start, GROUP, 0)
        k_block = lax.dynamic_slice_in_dim(k_rows, row_start, GROUP, 0)
        v_block = lax.dynamic_slice_in_dim(v_rows, row_start, GROUP, 0)
        grad_block = lax.dynamic_slice_in_dim(grad_out, row_start, GROUP, 0)
        held_state = lax.dynamic_index_in_dim(saved_states, block_idx, 0, keepdims=False)
        scores = lax.dynamic_index_in_dim(saved_scores, block_idx, 0, keepdims=False)
        grad_vals = jnp.where(causal, plain_product(grad_block, v_block.T), 0.0)
        query_part = plain_product(grad_block, held_state.T) + plain_product(grad_vals, k_block)
        key_part = leading_product(grad_vals, q_block) + plain_product(v_block, running.T)
        value_part = leading_product(scores, grad_block) + plain_product(k_block, running)
        grad_q = lax.dynamic_update_slice_in_dim(grad_q, query_part, row_start, 0)
        grad_k = lax.dynamic_update_slice_in_dim(grad_k, key_part, row_start, 0)
        grad_v = lax.dynamic_update_slice_in_dim(grad_v, value_part, row_start, 0)
        running = running + leading_product(q_block, grad_block)
        return (running, grad_q, grad_k, grad_v)

    zero_rows = jnp.zeros((capacity, features_dev), jnp.float32)
    shard_grad, grad_q, grad_k, grad_v = lax.fori_loop(
        0, block_live, backward_step, (zero_state, zero_rows, zero_rows, zero_rows)
    )
    piece_rows = lax.all_gather(shard_grad[None], "seq", axis=0, tiled=True)
    picked = (jnp.arange(piece_rows.shape[0]) > shard_pos)[:, None, None]
    state_out = jnp.sum(jnp.where(picked, piece_rows, 0.0), axis=0)
    grad_query = jnp.where(live_rows, grad_q + plain_product(grad_out, state_in.T), 0.0)
    grad_key = jnp.where(live_rows, grad_k + plain_product(v_rows, state_out.T), 0.0)
    grad_value = jnp.where(live_rows, grad_v + plain_product(k_rows, state_out), 0.0)
    return (normed, grad_query, grad_key, grad_value)


def solution(mesh):
    in_specs = (
        P("seq", "head"),
        P("seq", "head"),
        P("seq", "head"),
        P("seq", "head"),
        P("head"),
        P("head"),
        P(),
    )
    out_specs = (P("seq", "head"), P("seq", "head"), P("seq", "head"), P("seq", "head"))
    return jax.shard_map(
        on_device, mesh=mesh, in_specs=in_specs, out_specs=out_specs, check_vma=False
    )
```

profile of v0, /device:TPU:0, one launch (start us, length us, event | category | flops | bytes accessed | tf_op | source)
XLA Modules:
  0.0 95.1 jit_solution(258238342465137067)
XLA Ops:
  0.7 1.2 %copy.12 = f32[768,128]{0,1:T(8,128)S(1)} copy(f32[768,128]{1,0:T(8,128)} %param.14) | data formatting | bytes 786432 | tf_op args[3]
  2.6 0.6 copy-done.6
  3.2 0.7 dynamic_slice.43
  4.6 1.2 %broadcast_select_fusion = (f32[768,128]{1,0:T(8,128)S(1)}, f32[768,128]{1,0:T(8,128)S(1)}, f32[768,128]{1,0:T(8,128)S(1)}) fusion(f32[768,128]{1,0:T(8,128)} %param.11, pred[768]{0:T(1024)(128)(4,1)S(1)} %iota_compare_fusion.2, f32[768,128]{1,0:T(8,128)S(1)} %copy-done, f32[768,128]{1,0:T(8,128)S(1)} %copy-done.1), kind=kLoop, calls=%fused_computation.68 | loop fusion | flops 294912 | bytes 2360064 | tf_op jit(solution)/shard_map/jit(_where)/select_n | solution.py:28
  5.9 11.8 %while.36 = (s32[]{:T(128)}, f32[128,128]{1,0:T(8,128)S(1)}, f32[768,128]{0,1:T(8,128)S(1)}, f32[6,128,128]{2,1,0:T(8,128)S(1)}, f32[6,128,128]{2,1,0:T(8,128)S(...) while((s32[]{:T(128)}, f32[128,128]{1,0:T(8,128)S(1)}, ...), condition=%wide.region_1.2_spmd.clone, body=%wide.region_0.1_spmd.clone.sunk | while | flops 100728832 | bytes 1379053 | solution.py:55
  6.8 0.3 convolution_add_fusion.13
  8.7 0.3 convolution_add_fusion.13
  12.4 0.3 convolution_add_fusion.13
  14.3 0.3 convolution_add_fusion.13
  17.7 14.4 %all-gather = f32[512,128]{1,0:T(8,128)S(1)} all-gather(f32[128,128]{1,0:T(8,128)S(1)} %get-tuple-element.221), channel_id=2, replica_groups=mesh['seq'=4,'head'=8] {'seq'}, dimensions={0}, use_global_device_ids=true | all-gather | bytes 327680 | tf_op jit(solution)/shard_map/all_gather | solution.py:58
  32.2 0.6 copy-done.5
  32.8 0.6 multiply_reduce_fusion
  33.4 13.0 %all-reduce = (f32[768]{0:T(1024)S(1)}, f32[768]{0:T(1024)S(1)}) all-reduce(f32[768]{0:T(1024)S(1)} %get-tuple-element.296, f32[768]{0:T(1024)S(1)} %get-tuple-element.295), channel_id=1, replica_groups=mesh['seq'=4,'head'=8] {'head'}, use_global_device_ids=true, to_apply=%region_4.5 | all-reduce | flops 1536 | bytes 12288 | tf_op jit(solution)/shard_map/psum | solution.py:64
  46.5 0.9 copy.15
  48.2 28.3 %while.37 = (s32[]{:T(128)}, f32[128,128]{1,0:T(8,128)S(1)}, f32[768,128]{1,0:T(8,128)S(1)}, f32[768,128]{1,0:T(8,128)S(1)}, f32[768,128]{1,0:T(8,128)S(1)}, /*i...) while((s32[]{:T(128)}, f32[128,128]{1,0:T(8,128)S(1)}, ...), condition=%wide.region_8.9_spmd.clone, body=%wide.region_7.8_spmd.clone.sunk | while | flops 201424896 | bytes 1840413 | solution.py:97
  49.0 1.1 %fusion.115 = f32[128,128]{1,0:T(8,128)S(1)} fusion(f32[6,128,128]{2,1,0:T(8,128)} %get-tuple-element.581, s32[]{:T(128)S(6)} %select_n.105, f32[768,128]{0,1:T(8,128)S(1)} %get-tuple-element.577, s32[]{:T(128)S(6)} %select_n.104), kind=kOutput, calls=%fused_computation.28.clone.1 | convolution fusion | flops 25165824 | bytes 196616 | tf_op jit(solution)/shard_map/while/body/dot_general | solution.py:14
  51.5 1.1 %fusion.111 = f32[128,128]{1,0:T(8,128)S(1)} fusion(f32[6,128,128]{2,1,0:T(8,128)} %get-tuple-element.578, s32[]{:T(128)S(6)} %select_n.105, f32[768,128]{0,1:T(8,128)S(1)} %get-tuple-element.577, s32[]{:T(128)S(6)} %select_n.104), kind=kOutput, calls=%fused_computation.30.clone.1 | convolution fusion | flops 25165824 | bytes 196616 | tf_op jit(solution)/shard_map/while/body/dot_general | solution.py:10
  53.6 1.1 %fusion.115 = f32[128,128]{1,0:T(8,128)S(1)} fusion(f32[6,128,128]{2,1,0:T(8,128)} %get-tuple-element.581, s32[]{:T(128)S(6)} %select_n.105, f32[768,128]{0,1:T(8,128)S(1)} %get-tuple-element.577, s32[]{:T(128)S(6)} %select_n.104), kind=kOutput, calls=%fused_computation.28.clone.1 | convolution fusion | flops 25165824 | bytes 196616 | tf_op jit(solution)/shard_map/while/body/dot_general | solution.py:14
  56.1 1.1 %fusion.111 = f32[128,128]{1,0:T(8,128)S(1)} fusion(f32[6,128,128]{2,1,0:T(8,128)} %get-tuple-element.578, s32[]{:T(128)S(6)} %select_n.105, f32[768,128]{0,1:T(8,128)S(1)} %get-tuple-element.577, s32[]{:T(128)S(6)} %select_n.104), kind=kOutput, calls=%fused_computation.30.clone.1 | convolution fusion | flops 25165824 | bytes 196616 | tf_op jit(solution)/shard_map/while/body/dot_general | solution.py:10
  58.2 1.1 %fusion.115 = f32[128,128]{1,0:T(8,128)S(1)} fusion(f32[6,128,128]{2,1,0:T(8,128)} %get-tuple-element.581, s32[]{:T(128)S(6)} %select_n.105, f32[768,128]{0,1:T(8,128)S(1)} %get-tuple-element.577, s32[]{:T(128)S(6)} %select_n.104), kind=kOutput, calls=%fused_computation.28.clone.1 | convolution fusion | flops 25165824 | bytes 196616 | tf_op jit(solution)/shard_map/while/body/dot_general | solution.py:14
  59.5 0.3 convolution_select_fusion.3
  60.7 1.1 %fusion.111 = f32[128,128]{1,0:T(8,128)S(1)} fusion(f32[6,128,128]{2,1,0:T(8,128)} %get-tuple-element.578, s32[]{:T(128)S(6)} %select_n.105, f32[768,128]{0,1:T(8,128)S(1)} %get-tuple-element.577, s32[]{:T(128)S(6)} %select_n.104), kind=kOutput, calls=%fused_computation.30.clone.1 | convolution fusion | flops 25165824 | bytes 196616 | tf_op jit(solution)/shard_map/while/body/dot_general | solution.py:10
  62.8 1.1 %fusion.115 = f32[128,128]{1,0:T(8,128)S(1)} fusion(f32[6,128,128]{2,1,0:T(8,128)} %get-tuple-element.581, s32[]{:T(128)S(6)} %select_n.105, f32[768,128]{0,1:T(8,128)S(1)} %get-tuple-element.577, s32[]{:T(128)S(6)} %select_n.104), kind=kOutput, calls=%fused_computation.28.clone.1 | convolution fusion | flops 25165824 | bytes 196616 | tf_op jit(solution)/shard_map/while/body/dot_general | solution.py:14
  65.3 1.1 %fusion.111 = f32[128,128]{1,0:T(8,128)S(1)} fusion(f32[6,128,128]{2,1,0:T(8,128)} %get-tuple-element.578, s32[]{:T(128)S(6)} %select_n.105, f32[768,128]{0,1:T(8,128)S(1)} %get-tuple-element.577, s32[]{:T(128)S(6)} %select_n.104), kind=kOutput, calls=%fused_computation.30.clone.1 | convolution fusion | flops 25165824 | bytes 196616 | tf_op jit(solution)/shard_map/while/body/dot_general | solution.py:10
  67.4 1.1 %fusion.115 = f32[128,128]{1,0:T(8,128)S(1)} fusion(f32[6,128,128]{2,1,0:T(8,128)} %get-tuple-element.581, s32[]{:T(128)S(6)} %select_n.105, f32[768,128]{0,1:T(8,128)S(1)} %get-tuple-element.577, s32[]{:T(128)S(6)} %select_n.104), kind=kOutput, calls=%fused_computation.28.clone.1 | convolution fusion | flops 25165824 | bytes 196616 | tf_op jit(solution)/shard_map/while/body/dot_general | solution.py:14
  69.9 1.1 %fusion.111 = f32[128,128]{1,0:T(8,128)S(1)} fusion(f32[6,128,128]{2,1,0:T(8,128)} %get-tuple-element.578, s32[]{:T(128)S(6)} %select_n.105, f32[768,128]{0,1:T(8,128)S(1)} %get-tuple-element.577, s32[]{:T(128)S(6)} %select_n.104), kind=kOutput, calls=%fused_computation.30.clone.1 | convolution fusion | flops 25165824 | bytes 196616 | tf_op jit(solution)/shard_map/while/body/dot_general | solution.py:10
  72.0 1.1 %fusion.115 = f32[128,128]{1,0:T(8,128)S(1)} fusion(f32[6,128,128]{2,1,0:T(8,128)} %get-tuple-element.581, s32[]{:T(128)S(6)} %select_n.105, f32[768,128]{0,1:T(8,128)S(1)} %get-tuple-element.577, s32[]{:T(128)S(6)} %select_n.104), kind=kOutput, calls=%fused_computation.28.clone.1 | convolution fusion | flops 25165824 | bytes 196616 | tf_op jit(solution)/shard_map/while/body/dot_general | solution.py:14
  74.5 1.1 %fusion.111 = f32[128,128]{1,0:T(8,128)S(1)} fusion(f32[6,128,128]{2,1,0:T(8,128)} %get-tuple-element.578, s32[]{:T(128)S(6)} %select_n.105, f32[768,128]{0,1:T(8,128)S(1)} %get-tuple-element.577, s32[]{:T(128)S(6)} %select_n.104), kind=kOutput, calls=%fused_computation.30.clone.1 | convolution fusion | flops 25165824 | bytes 196616 | tf_op jit(solution)/shard_map/while/body/dot_general | solution.py:10
  76.5 1.5 %fusion.44 = f32[768,128]{1,0:T(8,128)} fusion(f32[768,128]{1,0:T(8,128)S(1)} %get-tuple-element.224, f32[768,128]{0,1:T(8,128)S(1)} %get-tuple-element.587, f32[128,128]{1,0:T(8,128)S(1)} %select_reduce_fusion.1, pred[768]{0:T(1024)(128)(4,1)S(1)} %iota_compare_fusion.2), kind=kOutput, calls=%fused_computation.59 | convolution fusion | flops 151191552 | bytes 1245952 | tf_op jit(solution)/shard_map/dot_general | solution.py:10
  78.1 14.4 %all-gather.1 = f32[512,128]{1,0:T(8,128)S(1)} all-gather(f32[128,128]{1,0:T(8,128)S(1)} %get-tuple-element.226), channel_id=3, replica_groups=mesh['seq'=4,'head'=8] {'seq'}, dimensions={0}, use_global_device_ids=true | all-gather | bytes 327680 | tf_op jit(solution)/shard_map/all_gather | solution.py:100
  92.6 1.3 %fusion.45 = f32[768,128]{1,0:T(8,128)} fusion(f32[768,128]{1,0:T(8,128)S(1)} %get-tuple-element.225, f32[128,128]{1,0:T(8,128)S(1)} %select_reduce_fusion, pred[768]{0:T(1024)(128)(4,1)S(1)} %iota_compare_fusion.2, f32[768,128]{1,0:T(8,128)S(1)} %copy-done), kind=kOutput, calls=%fused_computation.60 | convolution fusion | flops 151289856 | bytes 1245952 | tf_op jit(solution)/shard_map/dot_general | solution.py:10
  93.8 1.3 %fusion.46 = f32[768,128]{1,0:T(8,128)} fusion(f32[768,128]{1,0:T(8,128)S(1)} %get-tuple-element.227, f32[128,128]{1,0:T(8,128)S(1)} %select_reduce_fusion, pred[768]{0:T(1024)(128)(4,1)S(1)} %iota_compare_fusion.2, f32[768,128]{1,0:T(8,128)S(1)} %copy-done.2), kind=kOutput, calls=%fused_computation.61 | convolution fusion | flops 151289856 | bytes 1245952 | tf_op jit(solution)/shard_map/dot_general | solution.py:10
  (100 shorter events, 15.1 us)
Async XLA Ops:
  0.6 3.9 %copy-start = (f32[768,128]{1,0:T(8,128)S(1)}, f32[768,128]{1,0:T(8,128)}, u32[]{:S(2)}) copy-start(f32[768,128]{1,0:T(8,128)} %param.13) | copy-start | bytes 1179652
  0.6 3.9 %copy-start.1 = (f32[768,128]{1,0:T(8,128)S(1)}, f32[768,128]{1,0:T(8,128)}, u32[]{:S(2)}) copy-start(f32[768,128]{1,0:T(8,128)} %param.12) | copy-start | bytes 1179652
  2.5 0.7 copy-start.6
  17.7 14.4 %copy-start.3 = (f32[6,128,128]{2,1,0:T(8,128)}, f32[6,128,128]{2,1,0:T(8,128)S(1)}, u32[]{:S(2)}) copy-start(f32[6,128,128]{2,1,0:T(8,128)S(1)} %get-tuple-element.542) | copy-start | bytes 1179652
  17.7 15.6 %copy-start.4 = (f32[6,128,128]{2,1,0:T(8,128)}, f32[6,128,128]{2,1,0:T(8,128)S(1)}, u32[]{:S(2)}) copy-start(f32[6,128,128]{2,1,0:T(8,128)S(1)} %get-tuple-element.545) | copy-start | bytes 1179652
  32.1 0.7 copy-start.5
  92.6 1.3 %copy-start.2 = (f32[768,128]{1,0:T(8,128)S(1)}, f32[768,128]{1,0:T(8,128)}, u32[]{:S(2)}) copy-start(f32[768,128]{1,0:T(8,128)} %param.12) | copy-start | bytes 1179652
where the time goes:
time: 94.2 us; the launch traced here: 95.1 us
  blocking collectives  41.7 us (44%)
  matrix products  33.5 us (36%)
  loops' own time  10.6 us (11%)
  local copies, waits for them, and re-layouts  4.88 us (5%)
  between operations  2.89 us (3%)
  other arithmetic  1.52 us (2%)
    dot_general x52, matrix products, plain_product(): jnp.dot(left, right, precision=lax.Precision.HIGHEST, preferred_element_t...  21.5 us
    all_gather x1, blocking collectives, on_device(): piece_rows = lax.all_gather(shard_grad[None], 'seq', axis=0, tiled=True)  14.4 us
    all_gather x1, blocking collectives, on_device(): piece_rows = lax.all_gather(shard_state[None], 'seq', axis=0, tiled=True)  14.4 us
    psum x1, blocking collectives, on_device(): lax.psum((jnp.sum(scaled * scaled, axis=1), jnp.sum(norm_gain[None, :] *...  13 us
    dot_general x24, matrix products, leading_product(): lax.dot_general(left, right, (((0,), (0,)), ((), ())), precision=lax.Prec...  12 us
    another operation x1, loops' own time, on_device(): lax.fori_loop(0, block_live, backward_step, (zero_state, zero_rows, zero_...  5.32 us
    another operation x1, loops' own time, on_device(): lax.fori_loop(0, block_live, forward_step, forward_init)  5.26 us
    unnamed x16, local copies, waits for them, and re-layouts  3.38 us

commit v1 on v0

v1 whole, which is shorter than its diff:
```python
import functools

import jax
import jax.numpy as jnp
from jax import lax
from jax.experimental import pallas as pl
from jax.experimental.pallas import tpu as pltpu
from jax.sharding import PartitionSpec as P

GROUP = 128
CHUNKS = 4
EPS = 1e-05
F32 = jnp.float32
BF16 = jnp.bfloat16
NN = (((1,), (0,)), ((), ()))
NT = (((1,), (1,)), ((), ()))
TN = (((0,), (0,)), ((), ()))


def dot(left, right, dims):
    return lax.dot_general(left, right, dims, preferred_element_type=F32)


def split(x):
    high = x.astype(BF16)
    low = (x - high.astype(F32)).astype(BF16)
    return high, low


def rows_by_rows(a, b):
    left = jnp.concatenate([a[0], a[1], a[0]], axis=1)
    right = jnp.concatenate([b[0], b[0], b[1]], axis=1)
    return dot(left, right, NT)


def times(a, b):
    d = b[0].shape[1]
    both = dot(a[0], jnp.concatenate([b[0], b[1]], axis=1), NN)
    return both[:, :d] + both[:, d:] + dot(a[1], b[0], NN)


def times_state(a, s):
    d = s[0].shape[1]
    left = jnp.concatenate([a[0], a[1]], axis=1)
    top = jnp.concatenate([s[0], s[1]], axis=1)
    bottom = jnp.concatenate([s[0], jnp.zeros_like(s[0])], axis=1)
    both = dot(left, jnp.concatenate([top, bottom], axis=0), NN)
    return both[:, :d] + both[:, d:]


def times_state_t(a, s):
    d = s[0].shape[0]
    left = jnp.concatenate([a[0], a[1]], axis=1)
    top = jnp.concatenate([s[0], s[0]], axis=1)
    bottom = jnp.concatenate([s[1], jnp.zeros_like(s[1])], axis=1)
    both = dot(left, jnp.concatenate([top, bottom], axis=0), NT)
    return both[:, :d] + both[:, d:]


def outer(a, b):
    d = a[0].shape[1]
    full = dot(jnp.concatenate(a, axis=1), jnp.concatenate(b, axis=1), TN)
    return full[:d, :d] + full[:d, d:] + full[d:, :d] + full[d:, d:]


def row_sums(x):
    high, low = split(x)
    low2 = (x - high.astype(F32) - low.astype(F32)).astype(BF16)
    parts = jnp.concatenate([high, low, low2], axis=1)
    return dot(jnp.ones((8, parts.shape[1]), BF16), parts, NT)[0:1]


def kernel(
    n_seq, n_head, block, counts, head_scale,
    q_hbm, k_hbm, v_hbm, g_hbm, gain_hbm,
    normed_hbm, gq_hbm, gk_hbm, gv_hbm,
    q_in, k_in, v_in, g_in, gain,
    q_h, q_l, k_h, k_l, v_h, v_l, o_h, o_l, p_h, p_l,
    scaled, normed, gq, gk, gv,
    send_s, recv_s, send_t, recv_t, sums, sums_in,
    in_sem, out_sem, s_send, s_recv, t_send, t_recv, h_send, h_recv,
):
    cap, d = q_in.shape
    blocks = cap // block
    per = block // GROUP
    pos = lax.axis_index("seq")
    head = lax.axis_index("head")
    half = sums.shape[0] // 2

    loads = [
        pltpu.make_async_copy(src, dst, in_sem.at[i])
        for i, (src, dst) in enumerate(
            ((k_hbm, k_in), (v_hbm, v_in), (q_hbm, q_in), (g_hbm, g_in), (gain_hbm, gain))
        )
    ]
    for load in loads:
        load.start()

    first, last = pos == 0, pos == n_seq - 1
    barrier = pltpu.get_barrier_semaphore()

    @pl.when(jnp.logical_not(first))
    def _():
        pl.semaphore_signal(barrier, inc=1, device_id={"seq": pos - 1}, device_id_type=pl.DeviceIdType.MESH)

    @pl.when(jnp.logical_not(last))
    def _():
        pl.semaphore_signal(barrier, inc=1, device_id={"seq": pos + 1}, device_id_type=pl.DeviceIdType.MESH)

    for step in range(1, n_head):
        pl.semaphore_signal(
            barrier, inc=1, device_id={"head": lax.rem(head + step, n_head)},
            device_id_type=pl.DeviceIdType.MESH,
        )

    live = counts[pos] * GROUP
    row = lax.broadcasted_iota(jnp.int32, (block, d), 0)
    t_row = lax.broadcasted_iota(jnp.int32, (block, block), 0)
    t_col = lax.broadcasted_iota(jnp.int32, (block, block), 1)

    def take(b):
        return pl.ds(b * block, block)

    def pair(high, low, b):
        return high[take(b), :], low[take(b), :]

    def keep(source, high, low, b):
        x = jnp.where(row + b * block < live, source[take(b), :], 0.0)
        high[take(b), :], low[take(b), :] = split(x)

    sums[...] = jnp.zeros_like(sums)
    loads[0].wait()
    loads[1].wait()
    states = []
    for b in range(blocks):
        keep(k_in, k_h, k_l, b)
        keep(v_in, v_h, v_l, b)
        states.append(outer(pair(k_h, k_l, b), pair(v_h, v_l, b)))
    before = [jnp.zeros((d, d), F32)]
    for b in range(blocks):
        before.append(before[-1] + states[b])

    def piece(c):
        return pl.ds(c * (d // CHUNKS), d // CHUNKS)

    def hop(src, dst, s_sem, r_sem, c, target):
        return pltpu.make_async_remote_copy(
            src_ref=src.at[piece(c), :], dst_ref=dst.at[piece(c), :],
            send_sem=s_sem.at[c], recv_sem=r_sem.at[c],
            device_id={"seq": target}, device_id_type=pl.DeviceIdType.MESH,
        )

    send_s[...] = before[-1]
    pl.semaphore_wait(
        barrier,
        n_head - 1 + jnp.where(first, 0, 1) + jnp.where(last, 0, 1),
    )

    @pl.when(first)
    def _():
        for c in range(CHUNKS):
            hop(send_s, recv_s, s_send, s_recv, c, pos + 1).start()
        recv_s[...] = jnp.zeros_like(recv_s)

    loads[2].wait()
    for b in range(blocks):
        keep(q_in, q_h, q_l, b)
        q_b, k_b = pair(q_h, q_l, b), pair(k_h, k_l, b)
        scores = jnp.where(t_row >= t_col, rows_by_rows(q_b, k_b), 0.0)
        scaled[take(b), :] = times(split(scores), pair(v_h, v_l, b))

    @pl.when(jnp.logical_not(first))
    def _():
        for c in range(CHUNKS):
            hop(send_s, recv_s, s_send, s_recv, c, pos).wait_recv()

            @pl.when(jnp.logical_not(last))
            def _():
                send_s[piece(c), :] += recv_s[piece(c), :]
                hop(send_s, recv_s, s_send, s_recv, c, pos + 1).start()

    loads[3].wait()
    loads[4].wait()
    scale = head_scale[0]
    gains = gain[...].reshape(1, d)
    for b in range(blocks):
        state = recv_s[...] + before[b]
        mine = (scaled[take(b), :] + times_state(pair(q_h, q_l, b), split(state))) * scale
        scaled[take(b), :] = mine
        square = row_sums(mine * mine)
        cross = row_sums(gains * g_in[take(b), :] * mine)
        for j in range(per):
            sums[b * per + j : b * per + j + 1, :] = square[:, j * GROUP : (j + 1) * GROUP]
            sums[half + b * per + j : half + b * per + j + 1, :] = cross[:, j * GROUP : (j + 1) * GROUP]

    shares = [
        pltpu.make_async_remote_copy(
            src_ref=sums, dst_ref=sums_in.at[step - 1],
            send_sem=h_send.at[step - 1], recv_sem=h_recv.at[step - 1],
            device_id={"head": lax.rem(head + step, n_head)},
            device_id_type=pl.DeviceIdType.MESH,
        )
        for step in range(1, n_head)
    ]
    for share in shares:
        share.start()

    for b in range(blocks):
        q_b, k_b = pair(q_h, q_l, b), pair(k_h, k_l, b)
        scores_t = jnp.where(t_row <= t_col, rows_by_rows(k_b, q_b), 0.0)
        p_h[take(b), :], p_l[take(b), :] = split(scores_t)

    total = sums[...]
    for step in range(1, n_head):
        shares[step - 1].wait_recv()
        total = total + sums_in[step - 1]
    features = d * n_head
    inverse = lax.rsqrt(total[:half] / features + EPS)
    factor = inverse * inverse * inverse * total[half:] / features
    columns = jnp.transpose(jnp.concatenate([inverse, factor], axis=0))

    t_states = []
    for b in range(blocks):
        inv = jnp.concatenate(
            [jnp.broadcast_to(columns[:, b * per + j : b * per + j + 1], (GROUP, d)) for j in range(per)], axis=0
        )
        fac = jnp.concatenate(
            [jnp.broadcast_to(columns[:, half + b * per + j : half + b * per + j + 1], (GROUP, d)) for j in range(per)],
            axis=0,
        )
        mine = scaled[take(b), :]
        weight = inv * gains
        normed[take(b), :] = mine * weight
        grad = (weight * g_in[take(b), :] - mine * fac) * scale
        grad = jnp.where(row + b * block < live, grad, 0.0)
        o_h[take(b), :], o_l[take(b), :] = split(grad)
        t_states.append(outer(pair(q_h, q_l, b), pair(o_h, o_l, b)))
    after = [jnp.zeros((d, d), F32)]
    for b in range(blocks - 1, -1, -1):
        after.append(after[-1] + t_states[b])
    after = after[::-1]

    send_t[...] = after[0]

    @pl.when(last)
    def _():
        for c in range(CHUNKS):
            hop(send_t, recv_t, t_send, t_recv, c, pos - 1).start()
        recv_t[...] = jnp.zeros_like(recv_t)

    store_normed = pltpu.make_async_copy(normed, normed_hbm, out_sem.at[0])
    store_normed.start()
    for b in range(blocks):
        o_b, v_b = pair(o_h, o_l, b), pair(v_h, v_l, b)
        pulled = jnp.where(t_row >= t_col, rows_by_rows(o_b, v_b), 0.0)
        pulled_t = jnp.where(t_row <= t_col, rows_by_rows(v_b, o_b), 0.0)
        state = recv_s[...] + before[b]
        gq[take(b), :] = times_state_t(o_b, split(state)) + times(split(pulled), pair(k_h, k_l, b))
        gk[take(b), :] = times(split(pulled_t), pair(q_h, q_l, b))
        gv[take(b), :] = times(pair(p_h, p_l, b), o_b)
    store_gq = pltpu.make_async_copy(gq, gq_hbm, out_sem.at[1])
    store_gq.start()

    @pl.when(jnp.logical_not(last))
    def _():
        for c in range(CHUNKS):
            hop(send_t, recv_t, t_send, t_recv, c, pos).wait_recv()

            @pl.when(jnp.logical_not(first))
            def _():
                send_t[piece(c), :] += recv_t[piece(c), :]
                hop(send_t, recv_t, t_send, t_recv, c, pos - 1).start()

    for b in range(blocks):
        state = split(recv_t[...] + after[b + 1])
        gk[take(b), :] += times_state_t(pair(v_h, v_l, b), state)
        gv[take(b), :] += times_state(pair(k_h, k_l, b), state)
    store_gk = pltpu.make_async_copy(gk, gk_hbm, out_sem.at[2])
    store_gv = pltpu.make_async_copy(gv, gv_hbm, out_sem.at[3])
    store_gk.start()
    store_gv.start()

    for share in shares:
        share.wait_send()

    @pl.when(jnp.logical_not(last))
    def _():
        for c in range(CHUNKS):
            hop(send_s, recv_s, s_send, s_recv, c, pos + 1).wait_send()

    @pl.when(jnp.logical_not(first))
    def _():
        for c in range(CHUNKS):
            hop(send_t, recv_t, t_send, t_recv, c, pos - 1).wait_send()

    store_normed.wait()
    store_gq.wait()
    store_gk.wait()
    store_gv.wait()


def on_device(n_seq, n_head, query, key_in, value, out_grad, head_scale, norm_gain, group_counts):
    cap, d = query.shape
    block = 2 * GROUP if cap % (2 * GROUP) == 0 else GROUP
    half = -(-(cap // GROUP) // 8) * 8
    any_space = pl.BlockSpec(memory_space=pl.ANY)
    smem = pl.BlockSpec(memory_space=pltpu.SMEM)
    wide = pltpu.VMEM((cap, d), F32)
    narrow = pltpu.VMEM((cap, d), BF16)
    state = pltpu.VMEM((d, d), F32)
    return pl.pallas_call(
        functools.partial(kernel, n_seq, n_head, block),
        out_shape=[jax.ShapeDtypeStruct((cap, d), F32)] * 4,
        in_specs=[smem, smem] + [any_space] * 5,
        out_specs=[any_space] * 4,
        scratch_shapes=[wide] * 4 + [pltpu.VMEM((d,), F32)]
        + [narrow] * 8 + [pltpu.VMEM((cap, block), BF16)] * 2
        + [wide] * 5
        + [state] * 4
        + [pltpu.VMEM((2 * half, GROUP), F32), pltpu.VMEM((n_head - 1, 2 * half, GROUP), F32)]
        + [pltpu.SemaphoreType.DMA((5,)), pltpu.SemaphoreType.DMA((4,))]
        + [pltpu.SemaphoreType.DMA((CHUNKS,))] * 4
        + [pltpu.SemaphoreType.DMA((n_head - 1,))] * 2,
        compiler_params=pltpu.CompilerParams(
            collective_id=0, has_side_effects=True, vmem_limit_bytes=48 * 1024 * 1024
        ),
    )(group_counts, head_scale, query, key_in, value, out_grad, norm_gain)


def solution(mesh):
    rows = P("seq", "head")
    return jax.shard_map(
        functools.partial(on_device, mesh.shape["seq"], mesh.shape["head"]),
        mesh=mesh,
        in_specs=(rows, rows, rows, rows, P("head"), P("head"), P()),
        out_specs=(rows, rows, rows, rows),
        check_vma=False,
    )
```

time: 94.2 us -> 37.4 us (0.40); the launches traced: 95.1 us -> 37.1 us
  blocking collectives: 41.7 us -> 0 us
  matrix products: 33.5 us -> 0 us
  Pallas kernels: 0 us -> 28.8 us
  loops' own time: 10.6 us -> 0 us
  local copies, waits for them, and re-layouts: 4.88 us -> 6.97 us
  between operations: 2.89 us -> 1.35 us
  other arithmetic: 1.52 us -> 0 us
    dot_general x76 -> x0, matrix products: 33.5 us -> none  [the longest x52 21.5 us: plain_product(): jnp.dot(left, right, precision=lax.Precision.HIGHEST, preferred_element_t...]
    pallas_call x0 -> x1, Pallas kernels: none -> 28.8 us  [on_device(): pl.pallas_call(functools.partial(kernel, n_seq, n_head, block), out_shape...]
    all_gather x2 -> x0, blocking collectives: 28.7 us -> none  [the longest x1 14.4 us: on_device(): piece_rows = lax.all_gather(shard_grad[None], 'seq', axis=0, tiled=True)]
    psum x1 -> x0, blocking collectives: 13 us -> none  [on_device(): lax.psum((jnp.sum(scaled * scaled, axis=1), jnp.sum(norm_gain[None, :] *...]
    another operation x2 -> x0, loops' own time: 10.6 us -> none  [the longest x1 5.32 us: on_device(): lax.fori_loop(0, block_live, backward_step, (zero_state, zero_rows, zero_...]
    unnamed x16, local copies, waits for them, and re-layouts: 3.38 us -> 6.97 us
    select_n x1 -> x0, other arithmetic: 1.17 us -> none  [on_device(): q_rows = jnp.where(live_rows, query, 0.0)]
where the time goes in v1:
time: 37.4 us; the launch traced here: 37.1 us
  Pallas kernels  28.8 us (77%)
  local copies, waits for them, and re-layouts  6.97 us (19%)
  between operations  1.35 us (4%)
    pallas_call x1, Pallas kernels, on_device(): pl.pallas_call(functools.partial(kernel, n_seq, n_head, block), out_shape...  28.8 us
    unnamed x16, local copies, waits for them, and re-layouts  6.97 us

profile of v1, /device:TPU:0, one launch (start us, length us, event | category | flops | bytes accessed | tf_op | source)
XLA Modules:
  0.0 37.1 jit_solution(13903533657498789359)
XLA Ops:
  0.6 0.0 copy-start.4
  0.6 0.0 copy-start.5
  1.3 0.0 copy-done.4
  1.3 0.0 copy-done.5
  1.3 0.0 copy-start
  1.3 1.0 %copy-done = f32[768,128]{1,0:T(8,128)S(1)} copy-done((f32[768,128]{1,0:T(8,128)S(1)}, f32[768,128]{1,0:T(8,128)}, u32[]{:S(2)}) %copy-start) | copy-done | bytes 393240
  2.3 0.0 copy-start.1
  2.3 1.0 %copy-done.1 = f32[768,128]{1,0:T(8,128)S(1)} copy-done((f32[768,128]{1,0:T(8,128)S(1)}, f32[768,128]{1,0:T(8,128)}, u32[]{:S(2)}) %copy-start.1) | copy-done | bytes 393240
  3.3 0.0 copy-start.2
  3.3 1.0 %copy-done.2 = f32[768,128]{1,0:T(8,128)S(1)} copy-done((f32[768,128]{1,0:T(8,128)S(1)}, f32[768,128]{1,0:T(8,128)}, u32[]{:S(2)}) %copy-start.2) | copy-done | bytes 393240
  4.3 0.0 copy-start.3
  4.3 1.0 %copy-done.3 = f32[768,128]{1,0:T(8,128)S(1)} copy-done((f32[768,128]{1,0:T(8,128)S(1)}, f32[768,128]{1,0:T(8,128)}, u32[]{:S(2)}) %copy-start.3) | copy-done | bytes 393240
  5.3 28.8 %shard_map.102 = (f32[768,128]{1,0:T(8,128)S(1)}, f32[768,128]{1,0:T(8,128)S(1)}, f32[768,128]{1,0:T(8,128)S(1)}, f32[768,128]{1,0:T(8,128)S(1)}) custom-call(s32[4]{0:T(128)S(1)} %copy-done.4, f32[1]{0:T(128)S(6)} %copy.15.head_scale, f32[768,128]{1,0:T(8,128)S(1)} %copy-done, f32[768,128]{1,0:T(8,128)S(1)} %copy-done.1, f32[768,128]{1,0:T(8,128)S(1)} %copy-done.2, ...), custom_call_target="tpu_custom_call" | custom-call | tf_op jit(solution)/shard_map/pallas_call | solution.py:311
  34.1 0.7 %copy.16 = f32[768,128]{1,0:T(8,128)} copy(f32[768,128]{1,0:T(8,128)S(1)} %get-tuple-element.8) | data formatting | bytes 786432
  34.9 0.7 %copy.17 = f32[768,128]{1,0:T(8,128)} copy(f32[768,128]{1,0:T(8,128)S(1)} %get-tuple-element.9) | data formatting | bytes 786432
  35.6 0.7 %copy.18 = f32[768,128]{1,0:T(8,128)} copy(f32[768,128]{1,0:T(8,128)S(1)} %get-tuple-element.10) | data formatting | bytes 786432
  36.4 0.7 %copy.19 = f32[768,128]{1,0:T(8,128)} copy(f32[768,128]{1,0:T(8,128)S(1)} %get-tuple-element.11) | data formatting | bytes 786432
Async XLA Ops:
  0.6 0.7 %copy-start.4 = (s32[4]{0:T(128)S(1)}, s32[4]{0:T(128)}, u32[]{:S(2)}) copy-start(s32[4]{0:T(128)} %counts.1) | copy-start | bytes 52
  0.6 0.7 %copy-start.5 = (f32[128]{0:T(128)S(1)}, f32[128]{0:T(128)}, u32[]{:S(2)}) copy-start(f32[128]{0:T(128)} %gain_hbm.1) | copy-start | bytes 1540
  1.3 1.0 %copy-start = (f32[768,128]{1,0:T(8,128)S(1)}, f32[768,128]{1,0:T(8,128)}, u32[]{:S(2)}) copy-start(f32[768,128]{1,0:T(8,128)} %q_hbm.1) | copy-start | bytes 1179652
  2.3 1.0 %copy-start.1 = (f32[768,128]{1,0:T(8,128)S(1)}, f32[768,128]{1,0:T(8,128)}, u32[]{:S(2)}) copy-start(f32[768,128]{1,0:T(8,128)} %k_hbm.1) | copy-start | bytes 1179652
  3.3 1.0 %copy-start.2 = (f32[768,128]{1,0:T(8,128)S(1)}, f32[768,128]{1,0:T(8,128)}, u32[]{:S(2)}) copy-start(f32[768,128]{1,0:T(8,128)} %v_hbm.1) | copy-start | bytes 1179652
  4.3 1.0 %copy-start.3 = (f32[768,128]{1,0:T(8,128)S(1)}, f32[768,128]{1,0:T(8,128)}, u32[]{:S(2)}) copy-start(f32[768,128]{1,0:T(8,128)} %g_hbm.1) | copy-start | bytes 1179652

commit v2 on v1

--- a/solution.py
+++ b/solution.py
@@ -71,14 +71,13 @@
 
 
 def kernel(
-    n_seq, n_head, block, counts, head_scale,
+    n_seq, n_head, block, head_scale, counts_hbm,
     q_hbm, k_hbm, v_hbm, g_hbm, gain_hbm,
-    normed_hbm, gq_hbm, gk_hbm, gv_hbm,
-    q_in, k_in, v_in, g_in, gain,
-    q_h, q_l, k_h, k_l, v_h, v_l, o_h, o_l, p_h, p_l,
-    scaled, normed, gq, gk, gv,
-    send_s, recv_s, send_t, recv_t, sums, sums_in,
-    in_sem, out_sem, s_send, s_recv, t_send, t_recv, h_send, h_recv,
+    normed, gq, gk, gv, k_h, k_l, v_h, v_l, t_out,
+    counts, q_in, k_in, v_in, g_in, gain,
+    q_h, q_l, o_h, o_l, p_h, p_l,
+    scaled, send_s, recv_s, send_t, recv_t, sums, sums_in,
+    in_sem, s_send, s_recv, t_send, t_recv, h_send, h_recv,
 ):
     cap, d = q_in.shape
     blocks = cap // block
@@ -90,7 +89,10 @@
     loads = [
         pltpu.make_async_copy(src, dst, in_sem.at[i])
         for i, (src, dst) in enumerate(
-            ((k_hbm, k_in), (v_hbm, v_in), (q_hbm, q_in), (g_hbm, g_in), (gain_hbm, gain))
+            (
+                (counts_hbm, counts), (k_hbm, k_in), (v_hbm, v_in), (q_hbm, q_in),
+                (g_hbm, g_in), (gain_hbm, gain),
+            )
         )
     ]
     for load in loads:
@@ -113,6 +115,7 @@
             device_id_type=pl.DeviceIdType.MESH,
         )
 
+    loads[0].wait()
     live = counts[pos] * GROUP
     row = lax.broadcasted_iota(jnp.int32, (block, d), 0)
     t_row = lax.broadcasted_iota(jnp.int32, (block, block), 0)
@@ -129,8 +132,8 @@
         high[take(b), :], low[take(b), :] = split(x)
 
     sums[...] = jnp.zeros_like(sums)
-    loads[0].wait()
     loads[1].wait()
+    loads[2].wait()
     states = []
     for b in range(blocks):
         keep(k_in, k_h, k_l, b)
@@ -162,7 +165,7 @@
             hop(send_s, recv_s, s_send, s_recv, c, pos + 1).start()
         recv_s[...] = jnp.zeros_like(recv_s)
 
-    loads[2].wait()
+    loads[3].wait()
     for b in range(blocks):
         keep(q_in, q_h, q_l, b)
         q_b, k_b = pair(q_h, q_l, b), pair(k_h, k_l, b)
@@ -179,8 +182,8 @@
                 send_s[piece(c), :] += recv_s[piece(c), :]
                 hop(send_s, recv_s, s_send, s_recv, c, pos + 1).start()
 
-    loads[3].wait()
     loads[4].wait()
+    loads[5].wait()
     scale = head_scale[0]
     gains = gain[...].reshape(1, d)
     for b in range(blocks):
@@ -248,8 +251,6 @@
             hop(send_t, recv_t, t_send, t_recv, c, pos - 1).start()
         recv_t[...] = jnp.zeros_like(recv_t)
 
-    store_normed = pltpu.make_async_copy(normed, normed_hbm, out_sem.at[0])
-    store_normed.start()
     for b in range(blocks):
         o_b, v_b = pair(o_h, o_l, b), pair(v_h, v_l, b)
         pulled = jnp.where(t_row >= t_col, rows_by_rows(o_b, v_b), 0.0)
@@ -258,8 +259,6 @@
         gq[take(b), :] = times_state_t(o_b, split(state)) + times(split(pulled), pair(k_h, k_l, b))
         gk[take(b), :] = times(split(pulled_t), pair(q_h, q_l, b))
         gv[take(b), :] = times(pair(p_h, p_l, b), o_b)
-    store_gq = pltpu.make_async_copy(gq, gq_hbm, out_sem.at[1])
-    store_gq.start()
 
     @pl.when(jnp.logical_not(last))
     def _():
@@ -272,13 +271,7 @@
                 hop(send_t, recv_t, t_send, t_recv, c, pos - 1).start()
 
     for b in range(blocks):
-        state = split(recv_t[...] + after[b + 1])
-        gk[take(b), :] += times_state_t(pair(v_h, v_l, b), state)
-        gv[take(b), :] += times_state(pair(k_h, k_l, b), state)
-    store_gk = pltpu.make_async_copy(gk, gk_hbm, out_sem.at[2])
-    store_gv = pltpu.make_async_copy(gv, gv_hbm, out_sem.at[3])
-    store_gk.start()
-    store_gv.start()
+        t_out[b] = recv_t[...] + after[b + 1]
 
     for share in shares:
         share.wait_send()
@@ -293,38 +286,72 @@
         for c in range(CHUNKS):
             hop(send_t, recv_t, t_send, t_recv, c, pos - 1).wait_send()
 
-    store_normed.wait()
-    store_gq.wait()
-    store_gk.wait()
-    store_gv.wait()
+
+def finish(
+    block, normed, gq, gk, gv, k_h, k_l, v_h, v_l, t_in,
+    normed_hbm, gq_hbm, gk_hbm, gv_hbm, gk_all, gv_all, sem,
+):
+    blocks = t_in.shape[0]
+    stores = [
+        pltpu.make_async_copy(normed, normed_hbm, sem.at[2 * blocks]),
+        pltpu.make_async_copy(gq, gq_hbm, sem.at[2 * blocks + 1]),
+    ]
+    for store in stores:
+        store.start()
+    for b in range(blocks):
+        rows = pl.ds(b * block, block)
+        state = split(t_in[b])
+        gk_all[rows, :] = gk[rows, :] + times_state_t((v_h[rows, :], v_l[rows, :]), state)
+        gv_all[rows, :] = gv[rows, :] + times_state((k_h[rows, :], k_l[rows, :]), state)
+        for i, (src, dst) in enumerate(((gk_all, gk_hbm), (gv_all, gv_hbm))):
+            store = pltpu.make_async_copy(src.at[rows, :], dst.at[rows, :], sem.at[2 * b + i])
+            store.start()
+            stores.append(store)
+    for store in stores:
+        store.wait()
 
 
 def on_device(n_seq, n_head, query, key_in, value, out_grad, head_scale, norm_gain, group_counts):
     cap, d = query.shape
     block = 2 * GROUP if cap % (2 * GROUP) == 0 else GROUP
     half = -(-(cap // GROUP) // 8) * 8
-    any_space = pl.BlockSpec(memory_space=pl.ANY)
-    smem = pl.BlockSpec(memory_space=pltpu.SMEM)
+    blocks = cap // block
+    hbm = pl.BlockSpec(memory_space=pltpu.HBM)
+    vmem = pl.BlockSpec(memory_space=pltpu.VMEM)
     wide = pltpu.VMEM((cap, d), F32)
     narrow = pltpu.VMEM((cap, d), BF16)
     state = pltpu.VMEM((d, d), F32)
-    return pl.pallas_call(
+    rows = jax.ShapeDtypeStruct((cap, d), F32)
+    rows_low = jax.ShapeDtypeStruct((cap, d), BF16)
+    held = pl.pallas_call(
         functools.partial(kernel, n_seq, n_head, block),
-        out_shape=[jax.ShapeDtypeStruct((cap, d), F32)] * 4,
-        in_specs=[smem, smem] + [any_space] * 5,
-        out_specs=[any_space] * 4,
-        scratch_shapes=[wide] * 4 + [pltpu.VMEM((d,), F32)]
-        + [narrow] * 8 + [pltpu.VMEM((cap, block), BF16)] * 2
-        + [wide] * 5
+        out_shape=[rows] * 4 + [rows_low] * 4 + [jax.ShapeDtypeStruct((blocks, d, d), F32)],
+        in_specs=[pl.BlockSpec(memory_space=pltpu.SMEM)] + [hbm] * 6,
+        out_specs=[vmem] * 9,
+        scratch_shapes=[pltpu.SMEM(group_counts.shape, jnp.int32)]
+        + [wide] * 4 + [pltpu.VMEM((d,), F32)]
+        + [narrow] * 4 + [pltpu.VMEM((cap, block), BF16)] * 2
+        + [wide]
         + [state] * 4
         + [pltpu.VMEM((2 * half, GROUP), F32), pltpu.VMEM((n_head - 1, 2 * half, GROUP), F32)]
-        + [pltpu.SemaphoreType.DMA((5,)), pltpu.SemaphoreType.DMA((4,))]
+        + [pltpu.SemaphoreType.DMA((6,))]
         + [pltpu.SemaphoreType.DMA((CHUNKS,))] * 4
         + [pltpu.SemaphoreType.DMA((n_head - 1,))] * 2,
         compiler_params=pltpu.CompilerParams(
-            collective_id=0, has_side_effects=True, vmem_limit_bytes=48 * 1024 * 1024
+            collective_id=0, has_side_effects=True, vmem_limit_bytes=32 * 1024 * 1024
         ),
-    )(group_counts, head_scale, query, key_in, value, out_grad, norm_gain)
+    )(head_scale, *(
+        pltpu.with_memory_space_constraint(x, pltpu.HBM)
+        for x in (group_counts, query, key_in, value, out_grad, norm_gain)
+    ))
+    return pl.pallas_call(
+        functools.partial(finish, block),
+        out_shape=[rows] * 4,
+        in_specs=[vmem] * 9,
+        out_specs=[hbm] * 4,
+        scratch_shapes=[wide] * 2 + [pltpu.SemaphoreType.DMA((2 * blocks + 2,))],
+        compiler_params=pltpu.CompilerParams(vmem_limit_bytes=32 * 1024 * 1024),
+    )(*held)
 
 
 def solution(mesh):

time: 37.4 us -> 29.3 us (0.78)
  local copies, waits for them, and re-layouts: 6.97 us -> 0 us
  Pallas kernels: 28.8 us -> 27.9 us
    unnamed x16 -> x0, local copies, waits for them, and re-layouts: 6.97 us -> none
    pallas_call x1, Pallas kernels: 28.8 us -> 26.7 us  [on_device(): pl.pallas_call(functools.partial(kernel, n_seq, n_head, block), out_shape...]
    pallas_call x0 -> x1, Pallas kernels: none -> 1.21 us  [on_device(): pl.pallas_call(functools.partial(finish, block), out_shape=[rows] * 4, in...]
where the time goes in v2:
time: 29.3 us; the launch traced here: 29.2 us
  Pallas kernels  27.9 us (95%)
  between operations  1.29 us (4%)
    pallas_call x1, Pallas kernels, on_device(): pl.pallas_call(functools.partial(kernel, n_seq, n_head, block), out_shape...  26.7 us
    pallas_call x1, Pallas kernels, on_device(): pl.pallas_call(functools.partial(finish, block), out_shape=[rows] * 4, in...  1.21 us

profile of v2, /device:TPU:0, one launch (start us, length us, event | category | flops | bytes accessed | tf_op | source)
XLA Modules:
  0.0 29.2 jit_solution(11063017468766856047)
XLA Ops:
  1.3 26.7 %shard_map.102 = (f32[768,128]{1,0:T(8,128)S(1)}, f32[768,128]{1,0:T(8,128)S(1)}, f32[768,128]{1,0:T(8,128)S(1)}, f32[768,128]{1,0:T(8,128)S(1)}, bf16[768,128]{...) custom-call(f32[1]{0:T(128)S(6)} %copy.11.head_scale, ...), custom_call_target="tpu_custom_call" | custom-call | tf_op jit(solution)/shard_map/pallas_call | solution.py:326
  28.0 1.2 %shard_map.103 = (f32[768,128]{1,0:T(8,128)}, f32[768,128]{1,0:T(8,128)}, f32[768,128]{1,0:T(8,128)}, f32[768,128]{1,0:T(8,128)}) custom-call(f32[768,128]{1,0:T(8,128)S(1)} %get-tuple-element.13.normed, f32[768,128]{1,0:T(8,128)S(1)} %get-tuple-element.14.gq, f32[768,128]{1,0:T(8,128)S(1)} %get-tuple-element.15.gk, f32[768,128]{1,0:T(8,128)S(1)} %get-tuple-element.16.gv, ...), custom_call_target="tpu_custom_call" | custom-call | tf_op jit(solution)/shard_map/pallas_call | solution.py:347

commit v3 on v2

--- a/solution.py
+++ b/solution.py
@@ -76,8 +76,8 @@
     normed, gq, gk, gv, k_h, k_l, v_h, v_l, t_out,
     counts, q_in, k_in, v_in, g_in, gain,
     q_h, q_l, o_h, o_l, p_h, p_l,
-    scaled, send_s, recv_s, send_t, recv_t, sums, sums_in,
-    in_sem, s_send, s_recv, t_send, t_recv, h_send, h_recv,
+    scaled, send_s, recv_s, send_t, recv_t, end_s, end_t, sums, sums_in,
+    in_sem, s_send, s_recv, t_send, t_recv, h_send, h_recv, e_send, e_recv,
 ):
     cap, d = q_in.shape
     blocks = cap // block
@@ -101,13 +101,26 @@
     first, last = pos == 0, pos == n_seq - 1
     barrier = pltpu.get_barrier_semaphore()
 
-    @pl.when(jnp.logical_not(first))
-    def _():
-        pl.semaphore_signal(barrier, inc=1, device_id={"seq": pos - 1}, device_id_type=pl.DeviceIdType.MESH)
-
-    @pl.when(jnp.logical_not(last))
-    def _():
-        pl.semaphore_signal(barrier, inc=1, device_id={"seq": pos + 1}, device_id_type=pl.DeviceIdType.MESH)
+    direct = 2 < n_seq <= 4
+
+    def greet(other):
+        pl.semaphore_signal(barrier, inc=1, device_id={"seq": other}, device_id_type=pl.DeviceIdType.MESH)
+
+    if direct:
+        for step in range(1, n_seq):
+            greet(lax.rem(pos + step, n_seq))
+        seq_peers = n_seq - 1
+    else:
+
+        @pl.when(jnp.logical_not(first))
+        def _():
+            greet(pos - 1)
+
+        @pl.when(jnp.logical_not(last))
+        def _():
+            greet(pos + 1)
+
+        seq_peers = jnp.where(first, 0, 1) + jnp.where(last, 0, 1)
 
     for step in range(1, n_head):
         pl.semaphore_signal(
@@ -153,17 +166,76 @@
             device_id={"seq": target}, device_id_type=pl.DeviceIdType.MESH,
         )
 
+    def reach(src, dst, way, target, step):
+        return pltpu.make_async_remote_copy(
+            src_ref=src, dst_ref=dst, send_sem=e_send.at[way, step], recv_sem=e_recv.at[way],
+            device_id={"seq": target}, device_id_type=pl.DeviceIdType.MESH,
+        )
+
+    def exchange(way, src, dst, end, s_sem, r_sem):
+        delta = 1 if way == 0 else -1
+        order = pos if way == 0 else n_seq - 1 - pos
+        head_of_chain = 1 if direct else 0
+
+        def begin():
+            if direct:
+
+                @pl.when(order == 0)
+                def _():
+                    for step in range(n_seq - 1, 0, -1):
+                        reach(src, end, way, pos + delta * step, step).start()
+                    end[...] = jnp.zeros_like(end)
+
+            @pl.when(order == head_of_chain)
+            def _():
+                for c in range(CHUNKS):
+                    hop(src, dst, s_sem, r_sem, c, pos + delta).start()
+
+            @pl.when(order <= head_of_chain)
+            def _():
+                dst[...] = jnp.zeros_like(dst)
+
+        def relay():
+            @pl.when(order > head_of_chain)
+            def _():
+                for c in range(CHUNKS):
+                    hop(src, dst, s_sem, r_sem, c, pos).wait_recv()
+
+                    @pl.when(order < n_seq - 1)
+                    def _():
+                        src[piece(c), :] += dst[piece(c), :]
+                        hop(src, dst, s_sem, r_sem, c, pos + delta).start()
+
+        def arrive():
+            if direct:
+
+                @pl.when(order > 0)
+                def _():
+                    reach(src, end, way, pos, 0).wait_recv()
+                    dst[...] += end[...]
+
+        def close():
+            if direct:
+
+                @pl.when(order == 0)
+                def _():
+                    for step in range(n_seq - 1, 0, -1):
+                        reach(src, end, way, pos + delta * step, step).wait_send()
+
+            @pl.when(jnp.logical_and(order >= head_of_chain, order < n_seq - 1))
+            def _():
+                for c in range(CHUNKS):
+                    hop(src, dst, s_sem, r_sem, c, pos + delta).wait_send()
+
+        return begin, relay, arrive, close
+
+    s_begin, s_relay, s_arrive, s_close = exchange(0, send_s, recv_s, end_s, s_send, s_recv)
+    t_begin, t_relay, t_arrive, t_close = exchange(1, send_t, recv_t, end_t, t_send, t_recv)
+
     send_s[...] = before[-1]
-    pl.semaphore_wait(
-        barrier,
-        n_head - 1 + jnp.where(first, 0, 1) + jnp.where(last, 0, 1),
-    )
-
-    @pl.when(first)
-    def _():
-        for c in range(CHUNKS):
-            hop(send_s, recv_s, s_send, s_recv, c, pos + 1).start()
-        recv_s[...] = jnp.zeros_like(recv_s)
+    pl.semaphore_wait(barrier, n_head - 1 + seq_peers)
+
+    s_begin()
 
     loads[3].wait()
     for b in range(blocks):
@@ -172,15 +244,8 @@
         scores = jnp.where(t_row >= t_col, rows_by_rows(q_b, k_b), 0.0)
         scaled[take(b), :] = times(split(scores), pair(v_h, v_l, b))
 
-    @pl.when(jnp.logical_not(first))
-    def _():
-        for c in range(CHUNKS):
-            hop(send_s, recv_s, s_send, s_recv, c, pos).wait_recv()
-
-            @pl.when(jnp.logical_not(last))
-            def _():
-                send_s[piece(c), :] += recv_s[piece(c), :]
-                hop(send_s, recv_s, s_send, s_recv, c, pos + 1).start()
+    s_relay()
+    s_arrive()
 
     loads[4].wait()
     loads[5].wait()
@@ -245,12 +310,7 @@
 
     send_t[...] = after[0]
 
-    @pl.when(last)
-    def _():
-        for c in range(CHUNKS):
-            hop(send_t, recv_t, t_send, t_recv, c, pos - 1).start()
-        recv_t[...] = jnp.zeros_like(recv_t)
-
+    t_begin()
     for b in range(blocks):
         o_b, v_b = pair(o_h, o_l, b), pair(v_h, v_l, b)
         pulled = jnp.where(t_row >= t_col, rows_by_rows(o_b, v_b), 0.0)
@@ -260,31 +320,16 @@
         gk[take(b), :] = times(split(pulled_t), pair(q_h, q_l, b))
         gv[take(b), :] = times(pair(p_h, p_l, b), o_b)
 
-    @pl.when(jnp.logical_not(last))
-    def _():
-        for c in range(CHUNKS):
-            hop(send_t, recv_t, t_send, t_recv, c, pos).wait_recv()
-
-            @pl.when(jnp.logical_not(first))
-            def _():
-                send_t[piece(c), :] += recv_t[piece(c), :]
-                hop(send_t, recv_t, t_send, t_recv, c, pos - 1).start()
-
+    t_relay()
+    t_arrive()
     for b in range(blocks):
         t_out[b] = recv_t[...] + after[b + 1]
 
     for share in shares:
         share.wait_send()
 
-    @pl.when(jnp.logical_not(last))
-    def _():
-        for c in range(CHUNKS):
-            hop(send_s, recv_s, s_send, s_recv, c, pos + 1).wait_send()
-
-    @pl.when(jnp.logical_not(first))
-    def _():
-        for c in range(CHUNKS):
-            hop(send_t, recv_t, t_send, t_recv, c, pos - 1).wait_send()
+    s_close()
+    t_close()
 
 
 def finish(
@@ -332,11 +377,12 @@
         + [wide] * 4 + [pltpu.VMEM((d,), F32)]
         + [narrow] * 4 + [pltpu.VMEM((cap, block), BF16)] * 2
         + [wide]
-        + [state] * 4
+        + [state] * 6
         + [pltpu.VMEM((2 * half, GROUP), F32), pltpu.VMEM((n_head - 1, 2 * half, GROUP), F32)]
         + [pltpu.SemaphoreType.DMA((6,))]
         + [pltpu.SemaphoreType.DMA((CHUNKS,))] * 4
-        + [pltpu.SemaphoreType.DMA((n_head - 1,))] * 2,
+        + [pltpu.SemaphoreType.DMA((n_head - 1,))] * 2
+        + [pltpu.SemaphoreType.DMA((2, n_seq)), pltpu.SemaphoreType.DMA((2,))],
         compiler_params=pltpu.CompilerParams(
             collective_id=0, has_side_effects=True, vmem_limit_bytes=32 * 1024 * 1024
         ),

time: 29.3 us -> 26.6 us (0.908)
  Pallas kernels: 27.9 us -> 25.1 us
    pallas_call x1, Pallas kernels: 26.7 us -> 23.9 us  [on_device(): pl.pallas_call(functools.partial(kernel, n_seq, n_head, block), out_shape...]
where the time goes in v3:
time: 26.6 us; the launch traced here: 26.4 us
  Pallas kernels  25.1 us (94%)
  between operations  1.29 us (5%)
    pallas_call x1, Pallas kernels, on_device(): pl.pallas_call(functools.partial(kernel, n_seq, n_head, block), out_shape...  23.9 us
    pallas_call x1, Pallas kernels, on_device(): pl.pallas_call(functools.partial(finish, block), out_shape=[rows] * 4, in...  1.21 us

profile of v3, /device:TPU:0, one launch (start us, length us, event | category | flops | bytes accessed | tf_op | source)
XLA Modules:
  0.0 26.4 jit_solution(4875344064184555642)
XLA Ops:
  1.3 23.9 %shard_map.102 = (f32[768,128]{1,0:T(8,128)S(1)}, f32[768,128]{1,0:T(8,128)S(1)}, f32[768,128]{1,0:T(8,128)S(1)}, f32[768,128]{1,0:T(8,128)S(1)}, bf16[768,128]{...) custom-call(f32[1]{0:T(128)S(6)} %copy.11.head_scale, ...), custom_call_target="tpu_custom_call" | custom-call | tf_op jit(solution)/shard_map/pallas_call | solution.py:371
  25.2 1.2 %shard_map.103 = (f32[768,128]{1,0:T(8,128)}, f32[768,128]{1,0:T(8,128)}, f32[768,128]{1,0:T(8,128)}, f32[768,128]{1,0:T(8,128)}) custom-call(f32[768,128]{1,0:T(8,128)S(1)} %get-tuple-element.13.normed, f32[768,128]{1,0:T(8,128)S(1)} %get-tuple-element.14.gq, f32[768,128]{1,0:T(8,128)S(1)} %get-tuple-element.15.gk, f32[768,128]{1,0:T(8,128)S(1)} %get-tuple-element.16.gv, ...), custom_call_target="tpu_custom_call" | custom-call | tf_op jit(solution)/shard_map/pallas_call | solution.py:393

commit v4 on v3

--- a/solution.py
+++ b/solution.py
@@ -101,26 +101,20 @@
     first, last = pos == 0, pos == n_seq - 1
     barrier = pltpu.get_barrier_semaphore()
 
-    direct = 2 < n_seq <= 4
+    direct = n_seq == 4
 
     def greet(other):
         pl.semaphore_signal(barrier, inc=1, device_id={"seq": other}, device_id_type=pl.DeviceIdType.MESH)
 
-    if direct:
-        for step in range(1, n_seq):
-            greet(lax.rem(pos + step, n_seq))
-        seq_peers = n_seq - 1
-    else:
-
-        @pl.when(jnp.logical_not(first))
+    seq_peers = 0
+    for delta in (-2, -1, 1, 2):
+        there = jnp.logical_and(pos + delta >= 0, pos + delta < n_seq)
+
+        @pl.when(there)
         def _():
-            greet(pos - 1)
-
-        @pl.when(jnp.logical_not(last))
-        def _():
-            greet(pos + 1)
-
-        seq_peers = jnp.where(first, 0, 1) + jnp.where(last, 0, 1)
+            greet(pos + delta)
+
+        seq_peers = seq_peers + jnp.where(there, 1, 0)
 
     for step in range(1, n_head):
         pl.semaphore_signal(
@@ -166,71 +160,91 @@
             device_id={"seq": target}, device_id_type=pl.DeviceIdType.MESH,
         )
 
-    def reach(src, dst, way, target, step):
+    def far(src, dst, s_sem, r_sem, target):
         return pltpu.make_async_remote_copy(
-            src_ref=src, dst_ref=dst, send_sem=e_send.at[way, step], recv_sem=e_recv.at[way],
+            src_ref=src, dst_ref=dst, send_sem=s_sem, recv_sem=r_sem,
             device_id={"seq": target}, device_id_type=pl.DeviceIdType.MESH,
         )
+
+    def part(ref, c):
+        return ref.at[piece(c), :]
 
     def exchange(way, src, dst, end, s_sem, r_sem):
         delta = 1 if way == 0 else -1
         order = pos if way == 0 else n_seq - 1 - pos
-        head_of_chain = 1 if direct else 0
+        first, last = order == 0, order == n_seq - 1
+
+        def neighbour(c):
+            return hop(src, dst, s_sem, r_sem, c, pos + delta)
+
+        def skip(c):
+            return far(part(src, c), part(dst, c), e_send.at[way, c], r_sem.at[c], pos + 2 * delta)
+
+        def own():
+            return far(src, end, e_send.at[way, CHUNKS], e_recv.at[way, CHUNKS], pos + delta)
 
         def begin():
-            if direct:
-
-                @pl.when(order == 0)
-                def _():
-                    for step in range(n_seq - 1, 0, -1):
-                        reach(src, end, way, pos + delta * step, step).start()
-                    end[...] = jnp.zeros_like(end)
-
-            @pl.when(order == head_of_chain)
+            @pl.when(first)
             def _():
                 for c in range(CHUNKS):
-                    hop(src, dst, s_sem, r_sem, c, pos + delta).start()
-
-            @pl.when(order <= head_of_chain)
-            def _():
+                    neighbour(c).start()
                 dst[...] = jnp.zeros_like(dst)
 
+            if direct:
+
+                @pl.when(order == 2)
+                def _():
+                    own().start()
+
         def relay():
-            @pl.when(order > head_of_chain)
+            @pl.when(jnp.logical_not(first))
             def _():
                 for c in range(CHUNKS):
-                    hop(src, dst, s_sem, r_sem, c, pos).wait_recv()
-
-                    @pl.when(order < n_seq - 1)
+                    neighbour(c).wait_recv()
+
+                    @pl.when(order == 1 if direct else jnp.logical_not(last))
                     def _():
                         src[piece(c), :] += dst[piece(c), :]
-                        hop(src, dst, s_sem, r_sem, c, pos + delta).start()
-
-        def arrive():
+                        if direct:
+                            skip(c).start()
+                        else:
+                            neighbour(c).start()
+
+                if direct:
+
+                    @pl.when(order == 1)
+                    def _():
+                        for c in range(CHUNKS):
+                            neighbour(c).start()
+
             if direct:
 
-                @pl.when(order > 0)
+                @pl.when(last)
                 def _():
-                    reach(src, end, way, pos, 0).wait_recv()
+                    own().wait_recv()
                     dst[...] += end[...]
 
         def close():
-            if direct:
-
-                @pl.when(order == 0)
-                def _():
-                    for step in range(n_seq - 1, 0, -1):
-                        reach(src, end, way, pos + delta * step, step).wait_send()
-
-            @pl.when(jnp.logical_and(order >= head_of_chain, order < n_seq - 1))
+            @pl.when(order <= 1 if direct else jnp.logical_not(last))
             def _():
                 for c in range(CHUNKS):
-                    hop(src, dst, s_sem, r_sem, c, pos + delta).wait_send()
-
-        return begin, relay, arrive, close
-
-    s_begin, s_relay, s_arrive, s_close = exchange(0, send_s, recv_s, end_s, s_send, s_recv)
-    t_begin, t_relay, t_arrive, t_close = exchange(1, send_t, recv_t, end_t, t_send, t_recv)
+                    neighbour(c).wait_send()
+
+            if direct:
+
+                @pl.when(order == 1)
+                def _():
+                    for c in range(CHUNKS):
+                        skip(c).wait_send()
+
+                @pl.when(order == 2)
+                def _():
+                    own().wait_send()
+
+        return begin, relay, close
+
+    s_begin, s_relay, s_close = exchange(0, send_s, recv_s, end_s, s_send, s_recv)
+    t_begin, t_relay, t_close = exchange(1, send_t, recv_t, end_t, t_send, t_recv)
 
     send_s[...] = before[-1]
     pl.semaphore_wait(barrier, n_head - 1 + seq_peers)
@@ -245,7 +259,6 @@
         scaled[take(b), :] = times(split(scores), pair(v_h, v_l, b))
 
     s_relay()
-    s_arrive()
 
     loads[4].wait()
     loads[5].wait()
@@ -321,7 +334,6 @@
         gv[take(b), :] = times(pair(p_h, p_l, b), o_b)
 
     t_relay()
-    t_arrive()
     for b in range(blocks):
         t_out[b] = recv_t[...] + after[b + 1]
 
@@ -382,7 +394,7 @@
         + [pltpu.SemaphoreType.DMA((6,))]
         + [pltpu.SemaphoreType.DMA((CHUNKS,))] * 4
         + [pltpu.SemaphoreType.DMA((n_head - 1,))] * 2
-        + [pltpu.SemaphoreType.DMA((2, n_seq)), pltpu.SemaphoreType.DMA((2,))],
+        + [pltpu.SemaphoreType.DMA((2, CHUNKS + 1)), pltpu.SemaphoreType.DMA((2, CHUNKS + 1))],
         compiler_params=pltpu.CompilerParams(
             collective_id=0, has_side_effects=True, vmem_limit_bytes=32 * 1024 * 1024
         ),

time: 26.6 us -> 26.3 us (0.989)
  Pallas kernels: 25.1 us -> 24.8 us
    pallas_call x1, Pallas kernels: 23.9 us -> 23.6 us  [on_device(): pl.pallas_call(functools.partial(kernel, n_seq, n_head, block), out_shape...]
where the time goes in v4:
time: 26.3 us; the launch traced here: 26.1 us
  Pallas kernels  24.8 us (94%)
  between operations  1.29 us (5%)
    pallas_call x1, Pallas kernels, on_device(): pl.pallas_call(functools.partial(kernel, n_seq, n_head, block), out_shape...  23.6 us
    pallas_call x1, Pallas kernels, on_device(): pl.pallas_call(functools.partial(finish, block), out_shape=[rows] * 4, in...  1.2 us

profile of v4, /device:TPU:0, one launch (start us, length us, event | category | flops | bytes accessed | tf_op | source)
XLA Modules:
  0.0 26.1 jit_solution(5863390534256920617)
XLA Ops:
  1.3 23.6 %shard_map.102 = (f32[768,128]{1,0:T(8,128)S(1)}, f32[768,128]{1,0:T(8,128)S(1)}, f32[768,128]{1,0:T(8,128)S(1)}, f32[768,128]{1,0:T(8,128)S(1)}, bf16[768,128]{...) custom-call(f32[1]{0:T(128)S(6)} %copy.11.head_scale, ...), custom_call_target="tpu_custom_call" | custom-call | tf_op jit(solution)/shard_map/pallas_call | solution.py:383
  24.9 1.2 %shard_map.103 = (f32[768,128]{1,0:T(8,128)}, f32[768,128]{1,0:T(8,128)}, f32[768,128]{1,0:T(8,128)}, f32[768,128]{1,0:T(8,128)}) custom-call(f32[768,128]{1,0:T(8,128)S(1)} %get-tuple-element.13.normed, f32[768,128]{1,0:T(8,128)S(1)} %get-tuple-element.14.gq, f32[768,128]{1,0:T(8,128)S(1)} %get-tuple-element.15.gk, f32[768,128]{1,0:T(8,128)S(1)} %get-tuple-element.16.gv, ...), custom_call_target="tpu_custom_call" | custom-call | tf_op jit(solution)/shard_map/pallas_call | solution.py:405
